TPU v7x, 512 devices: a whole 4x8x8 slice. The times are simulated.
512 devices in a mesh: ctx: 32 (over x, y), tp: 16 (over z, core).
Axes of the slice: x: 4, y: 8, z: 8, core: 2. Of those that a mesh axis runs over, the one named last changes fastest.
Arguments:
- queries: bfloat16 [16384, 8192], P('ctx', 'tp'), may hold values from -1.796875 to 1.796875
- keys: bfloat16 [16384, 8192], P('ctx', 'tp'), may hold values from -1.796875 to 1.796875
- values: bfloat16 [16384, 8192], P('ctx', 'tp'), may hold values from -12 to 12
- log_decay: float32 [64, 16384], P('tp', 'ctx'), may hold values from -2 to 0
- gain: float32 [8192], P('tp'), may hold values from 0.1 to 1.9
- grad_out: bfloat16 [16384, 8192], P('ctx', 'tp'), may hold values from -5 to 5
Outputs:
- normed: bfloat16 [16384, 8192], P('ctx', 'tp')
- grad_queries: bfloat16 [16384, 8192], P('ctx', 'tp')
- grad_keys: bfloat16 [16384, 8192], P('ctx', 'tp')
- grad_values: bfloat16 [16384, 8192], P('ctx', 'tp')
All inputs are finite; a program needn't handle non-finite values.
Results may differ from a plain program's by a relative error of at most 0.0069.
Values sent between devices are 32-bit elements; how exact they have to be, the bound alone decides.
A program may use at most 64 MiB of HBM per device.

v0:
```python
import jax
import jax.numpy as jnp
from jax import lax
from jax.sharding import PartitionSpec as P

ATTENTION_HEADS = 64
E = 128
BLOCK = 512


EPSILON = 1e-05


def prefix(shard, axis, combine, identity, reverse):
    devices, place = (lax.axis_size(axis), lax.axis_index(axis))
    everything = jax.tree.map(lambda part: lax.all_gather(part, axis), shard)
    start = jax.tree.map(
        lambda part, zero: jnp.broadcast_to(jnp.asarray(zero, part.dtype), part.shape),
        shard,
        identity,
    )

    def lap(k, before):
        at = devices - 1 - k if reverse else k
        reached = at > place if reverse else at < place
        new = combine(before, jax.tree.map(lambda part: part[at], everything))
        return jax.tree.map(lambda a, b: jnp.where(reached, a, b), new, before)

    return lax.fori_loop(0, devices, lap, start)


def chain_states(earlier, later):
    return (earlier[0] * later[0], later[0][:, None, None] * earlier[1] + later[1])


def per_device(queries, keys, values, log_decay, gain, grad_out):
    heads = log_decay.shape[0]
    tok_rows = log_decay.shape[1]
    blocks = tok_rows // BLOCK
    shape_four = (blocks, BLOCK, heads, E)
    query_blk = queries.reshape(shape_four)
    key_blk = keys.reshape(shape_four)
    value_blk = values.reshape(shape_four)
    decay_blk = log_decay.reshape(heads, blocks, BLOCK).transpose(1, 0, 2)
    cumulative = jnp.cumsum(decay_blk, axis=2)
    totals = cumulative[:, :, -1]
    factors = jnp.exp(totals)
    row_pos = lax.broadcasted_iota(jnp.int32, (BLOCK, BLOCK), 0)
    col_pos = lax.broadcasted_iota(jnp.int32, (BLOCK, BLOCK), 1)
    causal = row_pos >= col_pos
    spread = cumulative[:, :, :, None] - cumulative[:, :, None, :]
    weights = jnp.exp(jnp.where(causal, spread, -1e30))
    scores = jnp.einsum("nthe,nshe->nhts", query_blk, key_blk, preferred_element_type=jnp.float32)
    probs = (scores * weights).astype(jnp.bfloat16)
    rise = jnp.exp(cumulative).transpose(0, 2, 1)[:, :, :, None]
    fall = jnp.exp(totals[:, :, None] - cumulative).transpose(0, 2, 1)[:, :, :, None]
    query_dec = (query_blk * rise).astype(jnp.bfloat16)
    key_dec = (key_blk * fall).astype(jnp.bfloat16)
    contrib = jnp.einsum("nshe,nshf->nhef", key_dec, value_blk, preferred_element_type=jnp.float32)
    local_state = jnp.zeros((heads, E, E), jnp.float32)
    block_id = 0
    local_state = factors[block_id][:, None, None] * local_state + contrib[block_id]
    device_decay = jnp.prod(factors, axis=0)
    identity = (jnp.ones_like(device_decay), jnp.zeros_like(local_state))
    incoming = prefix((device_decay, local_state), "ctx", chain_states, identity, False)[1]
    current = incoming
    block_id = 0
    entering = [current]
    state_half = jnp.stack(entering).astype(jnp.bfloat16)
    attended = jnp.einsum(
        "nhts,nshe->nthe", probs, value_blk, preferred_element_type=jnp.float32
    ) + jnp.einsum("nthe,nhef->nthf", query_dec, state_half, preferred_element_type=jnp.float32)
    attended = attended.reshape(tok_rows, heads * E)
    squares = jnp.sum(attended * attended, axis=1)
    scaled_grad = gain[None, :] * grad_out.astype(jnp.float32)
    crossed = jnp.sum(scaled_grad * attended, axis=1)
    square_total = lax.psum(squares, "tp")
    inverse = lax.rsqrt(square_total / (ATTENTION_HEADS * E) + EPSILON)
    normed = (gain[None, :] * attended * inverse[:, None]).astype(jnp.bfloat16)
    cross_total = lax.psum(crossed, "tp")
    d_attended = (
        inverse[:, None] * scaled_grad
        - attended * (inverse**3 * cross_total / (ATTENTION_HEADS * E))[:, None]
    ).astype(jnp.bfloat16)
    grad_blk = d_attended.reshape(shape_four)
    state_grad = jnp.einsum(
        "nthe,nthf->nhef", query_dec, grad_blk, preferred_element_type=jnp.float32
    )
    local_grad = jnp.zeros((heads, E, E), jnp.float32)
    for block_id in reversed(range(blocks)):
        local_grad = factors[block_id][:, None, None] * local_grad + state_grad[block_id]
    d_prob = jnp.einsum("nthe,nshe->nhts", grad_blk, value_blk, preferred_element_type=jnp.float32)
    d_scores = (d_prob * weights).astype(jnp.bfloat16)
    intra_q = jnp.einsum("nhts,nshe->nthe", d_scores, key_blk, preferred_element_type=jnp.float32)
    intra_k = jnp.einsum("nhts,nthe->nshe", d_scores, query_blk, preferred_element_type=jnp.float32)
    intra_v = jnp.einsum("nhts,nthe->nshe", probs, grad_blk, preferred_element_type=jnp.float32)
    grad_q = intra_q + rise * jnp.einsum(
        "nthf,nhef->nthe", grad_blk, state_half, preferred_element_type=jnp.float32
    )
    identity = (jnp.ones_like(device_decay), jnp.zeros_like(local_grad))
    outgoing = prefix((device_decay, local_grad), "ctx", chain_states, identity, True)[1]
    leaving = [outgoing] * blocks
    current = outgoing
    for block_id in reversed(range(blocks)):
        leaving[block_id] = current
        current = factors[block_id][:, None, None] * current + state_grad[block_id]
    leave_half = jnp.stack(leaving).astype(jnp.bfloat16)
    grad_k = intra_k + fall * jnp.einsum(
        "nshf,nhef->nshe", value_blk, leave_half, preferred_element_type=jnp.float32
    )
    grad_v = intra_v + jnp.einsum(
        "nshe,nhef->nshf", key_dec, leave_half, preferred_element_type=jnp.float32
    )
    return (
        normed,
        grad_q.reshape(tok_rows, heads * E).astype(jnp.bfloat16),
        grad_k.reshape(tok_rows, heads * E).astype(jnp.bfloat16),
        grad_v.reshape(tok_rows, heads * E).astype(jnp.bfloat16),
    )


def solution(mesh):
    in_specs = (
        P("ctx", "tp"),
        P("ctx", "tp"),
        P("ctx", "tp"),
        P("tp", "ctx"),
        P("tp"),
        P("ctx", "tp"),
    )
    out_specs = (P("ctx", "tp"), P("ctx", "tp"), P("ctx", "tp"), P("ctx", "tp"))
    return jax.shard_map(
        per_device, mesh=mesh, in_specs=in_specs, out_specs=out_specs, check_vma=False
    )
```

profile of v0, /device:TPU:1, one launch (start us, length us, event | category | flops | bytes accessed | tf_op | source)
XLA Modules:
  0.0 332.6 jit_solution(3207388615223060408)
XLA Ops:
  8.0 1.2 reduce-window.6
  10.1 2.5 convolution_add_fusion.3
  12.9 31.3 %all-gather = f32[32,4,1]{1,2,0:T(1,128)S(1)} all-gather(f32[1,4,1]{1,2,0:T(1,128)S(1)} %get-tuple-element.337), channel_id=2, replica_groups=mesh['ctx'=32,'tp'=16] {'ctx'}, dimensions={0}, use_global_device_ids=true | all-gather | bytes 528 | tf_op jit(solution)/shard_map/all_gather | solution.py:16
  45.4 1.4 multiply_convert_fusion.1
  46.8 1.4 copy-done.1
  49.0 71.4 %all-gather.6.cloned.1.call-done = f32[128,128,128]{2,1,0:T(8,128)} async-done(((f32[4,128,128]{2,1,0:T(8,128)}), f32[128,128,128]{2,1,0:T(8,128)}) %all-gather.6.cloned.1.call-update) | async-done | bytes 8388624 | tf_op jit(solution)/shard_map/all_gather | solution.py:16
  120.4 35.1 %while.30 = (s32[]{:T(128)}, f32[4,128,128]{2,1,0:T(8,128)S(1)}, s32[]{:T(128)}, f32[32,4]{1,0:T(8,128)S(1)}, f32[32,4,128,128]{3,2,1,0:T(8,128)}, /*index=5*/s32[]{:T(128)}, s32[]{:T(128)}) while((s32[]{:T(128)}, f32[4,128,128]{2,1,0:T(8,128)S(1)}, s32[]{:T(128)}, f32[32,4]{1,0:T(8,128)S(1)}, f32[32,4,128,128]{3,2,1,0:T(8,128)}, ...), condition=%wide.region_3.4_spmd.clone, body=%wide.region_2.3_spmd.clone.sunk | while | flops 262148 | bytes 786593 | solution.py:29
  121.5 1.1 fusion.51
  122.6 1.1 fusion.51
  123.7 1.1 fusion.51
  124.8 1.1 fusion.51
  125.9 1.1 fusion.51
  127.0 1.1 fusion.51
  128.1 1.1 fusion.51
  129.2 1.1 fusion.51
  130.3 1.1 fusion.51
  131.4 1.1 fusion.51
  132.5 1.1 fusion.51
  133.6 1.1 fusion.51
  134.7 1.1 fusion.51
  135.8 1.1 fusion.51
  136.9 1.1 fusion.51
  138.0 1.1 fusion.51
  139.1 1.1 fusion.51
  140.2 1.1 fusion.51
  141.3 1.1 fusion.51
  142.4 1.1 fusion.51
  143.5 1.1 fusion.51
  144.6 1.1 fusion.51
  145.6 1.1 fusion.51
  146.7 1.1 fusion.51
  147.8 1.1 fusion.51
  148.9 1.1 fusion.51
  150.0 1.1 fusion.51
  151.1 1.1 fusion.51
  152.2 1.1 fusion.51
  153.3 1.1 fusion.51
  154.4 1.1 fusion.51
  156.2 1.3 multiply_reduce_fusion
  157.5 25.4 %all-reduce = (f32[512]{0:T(512)S(1)}, f32[512]{0:T(512)S(1)}) all-reduce(f32[512]{0:T(512)S(1)} %get-tuple-element.340, f32[512]{0:T(512)S(1)} %multiply_reduce_fusion), channel_id=1, replica_groups=mesh['ctx'=32,'tp'=16] {'tp'}, use_global_device_ids=true, to_apply=%region_5.6 | all-reduce | flops 1024 | bytes 8192 | tf_op jit(solution)/shard_map/psum | solution.py:77
  182.9 2.3 subtract_convert_fusion
  185.3 1.3 copy.119
  187.6 2.4 multiply_convert_fusion
  190.9 1.1 fusion.7
  191.9 2.0 copy.109
  194.0 2.0 convolution_bitcast_fusion
  196.0 3.0 fusion.30
  199.0 87.3 %all-gather.8.cloned.1.call-done = f32[128,128,128]{2,1,0:T(8,128)} async-done(((f32[4,128,128]{2,1,0:T(8,128)}), f32[128,128,128]{2,1,0:T(8,128)}) %all-gather.8.cloned.1.call-update) | async-done | bytes 8388624 | tf_op jit(solution)/shard_map/all_gather | solution.py:16
  286.3 35.3 %while.31 = (s32[]{:T(128)}, f32[4,128,128]{2,1,0:T(8,128)S(1)}, s32[]{:T(128)}, f32[32,4]{1,0:T(8,128)S(1)}, f32[32,4,128,128]{3,2,1,0:T(8,128)}, /*index=5*/s32[]{:T(128)}, s32[]{:T(128)}, s32[]{:T(128)}, s32[]{:T(128)}) while((s32[]{:T(128)}, f32[4,128,128]{2,1,0:T(8,128)S(1)}, s32[]{:T(128)}, f32[32,4]{1,0:T(8,128)S(1)}, ...), condition=%wide.region_9.10_spmd.clone, body=%wide.region_8.9_spmd.clone.sunk | while | flops 262152 | bytes 786655 | solution.py:29
  287.4 1.1 fusion.52
  291.8 1.1 fusion.52
  292.9 1.1 fusion.52
  297.4 1.1 fusion.52
  298.5 1.1 fusion.52
  301.8 1.1 fusion.52
  302.9 1.1 fusion.52
  304.0 1.1 fusion.52
  307.3 1.1 fusion.52
  308.4 1.1 fusion.52
  312.8 1.1 fusion.52
  313.9 1.1 fusion.52
  318.3 1.1 fusion.52
  319.4 1.1 fusion.52
  321.6 1.8 fusion.8
  (134 shorter events, 29.5 us)
Async XLA Ops:
  7.2 2.9 copy-start
  7.2 37.2 %copy-start.5 = (bf16[512,512]{1,0:T(8,128)(2,1)S(1)}, bf16[512,512]{1,0:T(8,128)(2,1)}, u32[]{:S(2)}) copy-start(bf16[512,512]{1,0:T(8,128)(2,1)} %param.10) | copy-start | bytes 1572868
  7.2 113.2 %all-gather.6.cloned.1.call-start = ((), (), s32[]{:S(2)}) async-start(), calls=%async_computation | async-start | bytes 8650752 | tf_op jit(solution)/shard_map/all_gather | solution.py:16
  12.6 273.7 %all-gather.8.cloned.1.call-start = ((), (), s32[]{:S(2)}) async-start(), calls=%async_computation.1 | async-start | bytes 8650752 | tf_op jit(solution)/shard_map/all_gather | solution.py:16
  12.9 35.2 %copy-start.3 = (bf16[512,512]{1,0:T(8,128)(2,1)S(1)}, bf16[512,512]{1,0:T(8,128)(2,1)}, u32[]{:S(2)}) copy-start(bf16[512,512]{1,0:T(8,128)(2,1)} %param.12) | copy-start | bytes 1572868
  44.7 0.7 copy-start.6
  46.8 1.4 copy-start.1
  120.4 35.8 %copy-start.8 = (f32[512]{0:T(512)S(1)}, f32[512]{0:T(512)}, u32[]{:S(2)}) copy-start(f32[512]{0:T(512)} %param.14) | copy-start | bytes 6148
  156.2 31.4 %copy-start.7 = (pred[512,512]{1,0:T(8,128)(4,1)S(1)}, pred[512,512]{1,0:T(8,128)(4,1)}, u32[]{:S(2)}) copy-start(pred[512,512]{1,0:T(8,128)(4,1)} %copy-done.6) | copy-start | bytes 786436
  190.0 1.9 copy-start.2
  199.0 125.4 %copy-start.4 = (bf16[512,512]{1,0:T(8,128)(2,1)S(1)}, bf16[512,512]{1,0:T(8,128)(2,1)}, u32[]{:S(2)}) copy-start(bf16[512,512]{1,0:T(8,128)(2,1)} %param.12) | copy-start | bytes 1572868
Sparse Core Ops, SparseCore 0:
  12.7 107.6 all-gather.5
  187.7 98.5 all-gather.7
where the time goes:
time: 335 us; the launch traced here: 333 us
  waiting for transfers between devices  159 us (47%)
  other arithmetic  72.8 us (22%)
  blocking collectives  56.7 us (17%)
  matrix products  17.5 us (5%)
  between operations  14.3 us (4%)
  local copies, waits for them, and re-layouts  10.3 us (3%)
    all_gather x2, waiting for transfers between devices, prefix(): everything = jax.tree.map(lambda part: lax.all_gather(part, axis), shard)  159 us
    select_n x64, other arithmetic, lap(): return jax.tree.map(lambda a, b: jnp.where(reached, a, b), new, before)  67.6 us
    all_gather x1, blocking collectives, prefix(): everything = jax.tree.map(lambda part: lax.all_gather(part, axis), shard)  31.3 us
    psum x1, blocking collectives, per_device(): square_total = lax.psum(squares, 'tp')  25.4 us
  transfers between devices with their start and end apart: 2, of which 2 were waited for; matrix products, arithmetic and copies ran while one was open for 4% of the time, Pallas kernels for 0%

commit v1 on v0

v1 whole, which is shorter than its diff:
```python
import jax
import jax.numpy as jnp
from jax import lax
from jax.experimental import pallas as pl
from jax.experimental.pallas import tpu as pltpu
from jax.sharding import PartitionSpec as P

ATTENTION_HEADS = 64
E = 128
BLOCK = 512
EPSILON = 1e-05

X, Y, TP = 4, 8, 16
HEADS = ATTENTION_HEADS // TP
PART = HEADS * E // Y
TILE = 128
F32, BF16 = jnp.float32, jnp.bfloat16

NN = (((1,), (0,)), ((), ()))
NT = (((1,), (1,)), ((), ()))
TN = (((0,), (0,)), ((), ()))


def dot(a, b, dims):
    return lax.dot_general(a, b, dims, preferred_element_type=F32)


def columns(row, width=TILE):
    return jnp.transpose(jnp.broadcast_to(row, (width, row.shape[1])))


def kernel(
    q_in, k_in, v_in, decay_in, gain_in, grad_in,
    normed_out, gq_out, gk_out, gv_out,
    q, k, v, decay, gain, grad,
    normed, gq, gk, gv,
    cum, col, rise, fall, qdec, kdec, weights, probs, dscores,
    att, squares, crosses, datt, half, gk_part, gv_part,
    factor_send, factor_recv, row_factor,
    part_f, recv_f, rows_f, back_f, state_f,
    part_b, recv_b, rows_b, back_b, state_b,
    stats,
    load_sem, store_sem,
    factor_ssem, factor_rsem, row_ssem, row_rsem,
    part_ssem, part_rsem, rows_ssem, rows_rsem, back_ssem, back_rsem,
    stat_ssem, stat_rsem,
):
    ctx, tp = lax.axis_index("ctx"), lax.axis_index("tp")
    x, y = ctx // Y, ctx % Y

    loads = [
        pltpu.make_async_copy(src, dst, load_sem.at[n])
        for n, (src, dst) in enumerate(
            ((decay_in, decay), (k_in, k), (v_in, v), (q_in, q), (gain_in, gain), (grad_in, grad))
        )
    ]
    for load in loads:
        load.start()

    def along_y(step):
        return (y + step) % Y

    def along_x(step):
        return (x + step) % X

    def along_tp(step):
        return (tp + step) % TP

    Y_STEPS = (4, 3, 5, 2, 6, 1, 7)
    X_STEPS = (2, 1, 3)
    TP_STEPS = (8, 9, 7, 10, 6, 11, 5, 12, 4, 13, 3, 14, 2, 15, 1)

    barrier = pltpu.get_barrier_semaphore()
    for step in Y_STEPS:
        pl.semaphore_signal(
            barrier, 1, device_id=(x * Y + along_y(step), tp), device_id_type=pl.DeviceIdType.MESH
        )
    for step in X_STEPS:
        pl.semaphore_signal(
            barrier, 1, device_id=(along_x(step) * Y + y, tp), device_id_type=pl.DeviceIdType.MESH
        )
    for step in TP_STEPS:
        pl.semaphore_signal(
            barrier, 1, device_id=(ctx, along_tp(step)), device_id_type=pl.DeviceIdType.MESH
        )

    def remote(src, dst, ssem, rsem, to_ctx, to_tp):
        return pltpu.make_async_remote_copy(
            src_ref=src, dst_ref=dst, send_sem=ssem, recv_sem=rsem,
            device_id=(to_ctx, to_tp), device_id_type=pl.DeviceIdType.MESH,
        )

    def spread_y(source, target, ssem, rsem):
        copies = []
        for step in Y_STEPS:
            to = along_y(step)
            copies.append(
                remote(source(to), target.at[y], ssem.at[to], rsem.at[y], x * Y + to, tp)
            )
            copies[-1].start()
        return copies

    def spread_x(source, target, ssem, rsem):
        copies = []
        for step in X_STEPS:
            to = along_x(step)
            copies.append(
                remote(source, target.at[x], ssem.at[to], rsem.at[x], to * Y + y, tp)
            )
            copies[-1].start()
        return copies

    def arrived_y(target, rsem, ssem):
        for step in Y_STEPS:
            at = along_y(step)
            remote(target.at[at], target.at[at], ssem.at[at], rsem.at[at], x * Y + at, tp).wait_recv()

    def arrived_x(target, rsem, ssem):
        for step in X_STEPS:
            at = along_x(step)
            remote(target.at[at], target.at[at], ssem.at[at], rsem.at[at], at * Y + y, tp).wait_recv()

    sent = []

    loads[0].wait()
    tokens = lax.broadcasted_iota(jnp.int32, (BLOCK, BLOCK), 0)
    until = lax.broadcasted_iota(jnp.int32, (BLOCK, BLOCK), 1)
    upper = jnp.where(tokens <= until, 1.0, 0.0).astype(F32)
    cum[...] = lax.dot_general(
        decay[...], upper, NN, precision=lax.Precision.HIGHEST, preferred_element_type=F32
    )
    for h in range(HEADS):
        row = cum[h : h + 1, :]
        total = row[:, BLOCK - 1 : BLOCK]
        factor_send[h] = jnp.exp(jnp.broadcast_to(total, (1, TILE)))
        wide = columns(row)
        col[h] = wide
        rise[h] = jnp.exp(wide)
        fall[h] = jnp.exp(total - wide)
    loads[1].wait()
    loads[2].wait()
    for h in range(HEADS):
        lanes = slice(h * E, (h + 1) * E)
        kdec[:, lanes] = (k[:, lanes].astype(F32) * fall[h]).astype(BF16)
        contrib = dot(kdec[:, lanes], v[:, lanes], TN)
        part_f[2 * h] = contrib[:PART]
        part_f[2 * h + 1] = contrib[PART:]

    pl.semaphore_wait(barrier, Y + X + TP - 3)
    sent += spread_y(lambda to: factor_send.at[to // 2], factor_recv, factor_ssem, factor_rsem)
    sent += spread_y(lambda to: part_f.at[to], recv_f, part_ssem.at[0], part_rsem.at[0])
    factor_recv[y] = factor_send[y // 2]
    recv_f[y] = part_f[y]

    loads[3].wait()

    def inside(h, carry):
        lanes = pl.ds(pl.multiple_of(h * E, E), E)
        qdec[:, lanes] = (q[:, lanes].astype(F32) * rise[h]).astype(BF16)
        row = cum[pl.ds(h, 1), :]
        for r in range(BLOCK // TILE):
            rows, width = slice(r * TILE, (r + 1) * TILE), (r + 1) * TILE
            scores = dot(q[rows, lanes], k[:width, lanes], NT)
            mine = col[h, rows, :]
            pieces = []
            for c in range(r + 1):
                spread = mine - row[:, c * TILE : (c + 1) * TILE]
                if c == r:
                    down = lax.broadcasted_iota(jnp.int32, (TILE, TILE), 0)
                    across = lax.broadcasted_iota(jnp.int32, (TILE, TILE), 1)
                    spread = jnp.where(down >= across, spread, -1e30)
                pieces.append(jnp.exp(spread))
            weight = pieces[0] if r == 0 else jnp.concatenate(pieces, axis=1)
            weights[h, rows, :width] = weight
            prob = (scores * weight).astype(BF16)
            probs[h, rows, :width] = prob
            att[rows, lanes] = dot(prob, v[:width, lanes], NN)
        return carry

    lax.fori_loop(0, HEADS, inside, 0)

    arrived_y(factor_recv, factor_rsem, factor_ssem)
    product = factor_recv[0]
    for j in range(1, Y):
        product = product * factor_recv[j]
    row_factor[x] = product
    sent += spread_x(row_factor.at[x], row_factor, row_ssem, row_rsem)

    def chain(order_y, order_x, before, recv, rows, back, state, n):
        running = recv[order_y[0]]
        back[order_y[0]] = jnp.zeros((PART, E), F32)
        for j in order_y[1:]:
            back[j] = running
            running = factor_recv[j] * running + recv[j]
        rows[x] = running
        copies = spread_x(rows.at[x], rows, rows_ssem.at[n], rows_rsem.at[n])
        if n == 0:
            arrived_x(row_factor, row_rsem, row_ssem)
        arrived_x(rows, rows_rsem.at[n], rows_ssem.at[n])
        enter = jnp.zeros((PART, E), F32)
        for i in order_x[:-1]:
            enter = jnp.where(before(i), row_factor[i] * enter + rows[i], enter)
        passed = enter
        for j in order_y:
            back[j] = back[j] + passed
            passed = factor_recv[j] * passed
        copies += spread_y(lambda to: back.at[to], state, back_ssem.at[n], back_rsem.at[n])
        state[y] = back[y]
        return copies

    arrived_y(recv_f, part_rsem.at[0], part_ssem.at[0])
    sent += chain(
        list(range(Y)), list(range(X)), lambda i: i < x, recv_f, rows_f, back_f, state_f, 0
    )
    loads[4].wait()
    loads[5].wait()
    arrived_y(state_f, back_rsem.at[0], back_ssem.at[0])

    def across(h, carry):
        lanes = pl.ds(pl.multiple_of(h * E, E), E)
        entering = state_f[pl.ds(2 * h, 2)].reshape(E, E).astype(BF16)
        half[h] = entering
        whole = att[:, lanes] + dot(qdec[:, lanes], entering, NN)
        att[:, lanes] = whole
        cotangent = gain[:, lanes] * grad[:, lanes].astype(F32)
        first = h == 0
        squares[...] = jnp.where(first, 0.0, squares[...]) + whole * whole
        crosses[...] = jnp.where(first, 0.0, crosses[...]) + cotangent * whole
        return carry

    squares[...] = jnp.zeros((BLOCK, E), F32)
    crosses[...] = jnp.zeros((BLOCK, E), F32)
    lax.fori_loop(0, HEADS, across, 0)

    own = jnp.concatenate(
        [
            jnp.sum(jnp.transpose(squares[...]), axis=0, keepdims=True),
            jnp.sum(jnp.transpose(crosses[...]), axis=0, keepdims=True),
        ],
        axis=0,
    )
    stats[tp] = own
    for step in TP_STEPS:
        to = along_tp(step)
        sent.append(
            remote(stats.at[tp], stats.at[tp], stat_ssem.at[to], stat_rsem.at[tp], ctx, to)
        )
        sent[-1].start()
    for step in TP_STEPS:
        at = along_tp(step)
        remote(stats.at[at], stats.at[at], stat_ssem.at[at], stat_rsem.at[at], ctx, at).wait_recv()
    sums = stats[0]
    for i in range(1, TP):
        sums = sums + stats[i]
    inverse_row = lax.rsqrt(sums[0:1] / (ATTENTION_HEADS * E) + EPSILON)
    slope_row = inverse_row * inverse_row * inverse_row * sums[1:2] / (ATTENTION_HEADS * E)
    squares[...] = columns(inverse_row)
    crosses[...] = columns(slope_row)

    def cotangents(h, carry):
        lanes = pl.ds(pl.multiple_of(h * E, E), E)
        inverse = squares[...]
        whole = att[:, lanes]
        scale = gain[:, lanes]
        here = (
            inverse * (scale * grad[:, lanes].astype(F32)) - whole * crosses[...]
        ).astype(BF16)
        datt[:, lanes] = here
        part_b[pl.ds(2 * h, 2)] = dot(qdec[:, lanes], here, TN).reshape(2, PART, E)
        return carry

    lax.fori_loop(0, HEADS, cotangents, 0)
    sent += spread_y(lambda to: part_b.at[to], recv_b, part_ssem.at[1], part_rsem.at[1])
    recv_b[y] = part_b[y]

    def backward(h, carry):
        lanes = pl.ds(pl.multiple_of(h * E, E), E)
        normed[:, lanes] = (gain[:, lanes] * att[:, lanes] * squares[...]).astype(BF16)
        entering = half[h]
        for r in range(BLOCK // TILE):
            rows, width = slice(r * TILE, (r + 1) * TILE), (r + 1) * TILE
            here = datt[rows, lanes]
            dprob = dot(here, v[:width, lanes], NT)
            dscore = (dprob * weights[h, rows, :width]).astype(BF16)
            dscores[h, rows, :width] = dscore
            gq[rows, lanes] = (
                dot(dscore, k[:width, lanes], NN) + rise[h, rows, :] * dot(here, entering, NT)
            ).astype(BF16)
        for c in range(BLOCK // TILE):
            place, later = slice(c * TILE, (c + 1) * TILE), slice(c * TILE, BLOCK)
            gk_part[place, lanes] = dot(dscores[h, later, place], q[later, lanes], TN)
            gv_part[place, lanes] = dot(probs[h, later, place], datt[later, lanes], TN)
        return carry

    lax.fori_loop(0, HEADS, backward, 0)
    stores = [
        pltpu.make_async_copy(src, dst, store_sem.at[n])
        for n, (src, dst) in enumerate(
            ((normed, normed_out), (gq, gq_out), (gk, gk_out), (gv, gv_out))
        )
    ]
    stores[0].start()
    stores[1].start()

    arrived_y(recv_b, part_rsem.at[1], part_ssem.at[1])
    sent += chain(
        list(reversed(range(Y))), list(reversed(range(X))), lambda i: i > x,
        recv_b, rows_b, back_b, state_b, 1,
    )
    arrived_y(state_b, back_rsem.at[1], back_ssem.at[1])

    def finish(h, carry):
        lanes = pl.ds(pl.multiple_of(h * E, E), E)
        leaving = state_b[pl.ds(2 * h, 2)].reshape(E, E).astype(BF16)
        gk[:, lanes] = (
            gk_part[:, lanes] + fall[h] * dot(v[:, lanes], leaving, NT)
        ).astype(BF16)
        gv[:, lanes] = (gv_part[:, lanes] + dot(kdec[:, lanes], leaving, NN)).astype(BF16)
        return carry

    lax.fori_loop(0, HEADS, finish, 0)
    stores[2].start()
    stores[3].start()
    for copy in sent:
        copy.wait_send()
    for store in stores:
        store.wait()


def per_device(queries, keys, values, log_decay, gain, grad_out):
    tile = jax.ShapeDtypeStruct((BLOCK, HEADS * E), BF16)
    flat16 = pltpu.VMEM((BLOCK, HEADS * E), BF16)
    flat32 = pltpu.VMEM((BLOCK, HEADS * E), F32)
    head32 = pltpu.VMEM((HEADS, BLOCK, E), F32)
    one32 = pltpu.VMEM((BLOCK, E), F32)
    square = (HEADS, BLOCK, BLOCK)
    parts = pltpu.VMEM((Y, PART, E), F32)
    across = pltpu.VMEM((X, PART, E), F32)
    sem = pltpu.SemaphoreType.DMA
    chain = [parts, parts, across, parts, parts]
    anywhere = pl.BlockSpec(memory_space=pl.ANY)
    return pl.pallas_call(
        kernel,
        out_shape=(tile,) * 4,
        in_specs=[anywhere] * 6,
        out_specs=(anywhere,) * 4,
        scratch_shapes=[
            flat16, flat16, flat16,
            pltpu.VMEM((HEADS, BLOCK), F32), pltpu.VMEM((1, HEADS * E), F32), flat16,
            flat16, flat16, flat16, flat16,
            pltpu.VMEM((HEADS, BLOCK), F32), head32, head32, head32, flat16, flat16,
            pltpu.VMEM(square, F32), pltpu.VMEM(square, BF16), pltpu.VMEM(square, BF16),
            flat32, one32, one32, flat16, pltpu.VMEM((HEADS, E, E), BF16), flat32, flat32,
            pltpu.VMEM((HEADS, 1, TILE), F32), pltpu.VMEM((Y, 1, TILE), F32),
            pltpu.VMEM((X, 1, TILE), F32),
            *chain, *chain,
            pltpu.VMEM((TP, 2, BLOCK), F32),
            sem((6,)), sem((4,)),
            sem((Y,)), sem((Y,)), sem((X,)), sem((X,)),
            sem((2, Y)), sem((2, Y)), sem((2, X)), sem((2, X)), sem((2, Y)), sem((2, Y)),
            sem((TP,)), sem((TP,)),
        ],
        compiler_params=pltpu.CompilerParams(collective_id=0, has_side_effects=True),
        name="layer",
    )(queries, keys, values, log_decay, gain.reshape(1, -1), grad_out)


def solution(mesh):
    in_specs = (
        P("ctx", "tp"),
        P("ctx", "tp"),
        P("ctx", "tp"),
        P("tp", "ctx"),
        P("tp"),
        P("ctx", "tp"),
    )
    out_specs = (P("ctx", "tp"), P("ctx", "tp"), P("ctx", "tp"), P("ctx", "tp"))
    return jax.shard_map(
        per_device, mesh=mesh, in_specs=in_specs, out_specs=out_specs, check_vma=False
    )
```

time: 335 us -> 68.1 us (0.20)
  waiting for transfers between devices: 159 us -> 0 us
  other arithmetic: 72.8 us -> 0 us
  Pallas kernels: 0 us -> 62 us
  blocking collectives: 56.7 us -> 0 us
  matrix products: 17.5 us -> 0 us
  between operations: 14.3 us -> 0.65 us
  local copies, waits for them, and re-layouts: 10.3 us -> 5.18 us
    all_gather x2 -> x0, waiting for transfers between devices: 159 us -> none  [prefix(): everything = jax.tree.map(lambda part: lax.all_gather(part, axis), shard)]
    select_n x64 -> x0, other arithmetic: 67.6 us -> none  [lap(): return jax.tree.map(lambda a, b: jnp.where(reached, a, b), new, before)]
    pallas_call x0 -> x1, Pallas kernels: none -> 62 us  [per_device(): pl.pallas_call(kernel, out_shape=(tile,) * 4, in_specs=[anywhere] * 6, ou...]
    all_gather x1 -> x0, blocking collectives: 31.3 us -> none  [prefix(): everything = jax.tree.map(lambda part: lax.all_gather(part, axis), shard)]
    psum x1 -> x0, blocking collectives: 25.4 us -> none  [per_device(): square_total = lax.psum(squares, 'tp')]
    dot_general x12 -> x0, matrix products: 17.5 us -> none  [the longest x1 3.01 us: per_device(): jnp.einsum('nhts,nthe->nshe', probs, grad_blk, preferred_element_type=jnp...]
  transfers between devices with their start and end apart: 2 -> 0, of which waited for: 2 -> 0; matrix products, arithmetic and copies ran while one was open for 4% -> 0% of each run, Pallas kernels for 0% -> 0%
where the time goes in v1:
time: 68.1 us; the launch traced here: 67.9 us
  Pallas kernels  62 us (91%)
  local copies, waits for them, and re-layouts  5.18 us (8%)
    pallas_call x1, Pallas kernels, per_device(): pl.pallas_call(kernel, out_shape=(tile,) * 4, in_specs=[anywhere] * 6, ou...  62 us
    unnamed x10, local copies, waits for them, and re-layouts  5.18 us

profile of v1, /device:TPU:1, one launch (start us, length us, event | category | flops | bytes accessed | tf_op | source)
XLA Modules:
  0.0 67.9 jit_solution(15913980280435801944)
XLA Ops:
  0.6 62.0 %layer.1 = (bf16[512,512]{1,0:T(8,128)(2,1)}, bf16[512,512]{1,0:T(8,128)(2,1)}, bf16[512,512]{1,0:T(8,128)(2,1)}, bf16[512,512]{1,0:T(8,128)(2,1)}) custom-call(bf16[512,512]{1,0:T(8,128)(2,1)} %q_in.1, bf16[512,512]{1,0:T(8,128)(2,1)} %k_in.1, bf16[512,512]{1,0:T(8,128)(2,1)} %v_in.1, f32[4,512]{1,0:T(4,128)} %decay_in.1, f32[1,512]{1,0:T(1,128)} %bitcast.1, ...), custom_call_target="tpu_custom_call" | custom-call | tf_op jit(solution)/shard_map/layer/pallas_call | solution.py:342
  62.7 0.0 copy-start.2
  62.7 1.9 %copy.14 = bf16[512,512]{1,0:T(8,128)(2,1)} copy(bf16[512,512]{1,0:T(8,128)(2,1)} %get-tuple-element.8) | data formatting | bytes 1048576
  64.6 0.0 copy-done.2
  64.6 0.0 copy-start.1
  64.6 0.8 %copy.15 = bf16[512,512]{1,0:T(8,128)(2,1)} copy(bf16[512,512]{1,0:T(8,128)(2,1)S(1)} %copy-done.2) | data formatting | bytes 1048576
  65.4 0.4 copy-done.1
  65.9 0.0 copy-start
  65.9 0.8 %copy.16 = bf16[512,512]{1,0:T(8,128)(2,1)} copy(bf16[512,512]{1,0:T(8,128)(2,1)S(1)} %copy-done.1) | data formatting | bytes 1048576
  66.6 0.4 copy-done
  67.1 0.8 %copy.17 = bf16[512,512]{1,0:T(8,128)(2,1)} copy(bf16[512,512]{1,0:T(8,128)(2,1)S(1)} %copy-done) | data formatting | bytes 1048576
Async XLA Ops:
  62.7 1.9 %copy-start.2 = (bf16[512,512]{1,0:T(8,128)(2,1)S(1)}, bf16[512,512]{1,0:T(8,128)(2,1)}, u32[]{:S(2)}) copy-start(bf16[512,512]{1,0:T(8,128)(2,1)} %get-tuple-element.9) | copy-start | bytes 1572868
  64.6 1.2 %copy-start.1 = (bf16[512,512]{1,0:T(8,128)(2,1)S(1)}, bf16[512,512]{1,0:T(8,128)(2,1)}, u32[]{:S(2)}) copy-start(bf16[512,512]{1,0:T(8,128)(2,1)} %get-tuple-element.10) | copy-start | bytes 1572868
  65.9 1.2 %copy-start = (bf16[512,512]{1,0:T(8,128)(2,1)S(1)}, bf16[512,512]{1,0:T(8,128)(2,1)}, u32[]{:S(2)}) copy-start(bf16[512,512]{1,0:T(8,128)(2,1)} %get-tuple-element.11) | copy-start | bytes 1572868

commit v2 on v1

--- a/solution.py
+++ b/solution.py
@@ -12,7 +12,8 @@
 
 X, Y, TP = 4, 8, 16
 HEADS = ATTENTION_HEADS // TP
-PART = HEADS * E // Y
+PART = E // Y
+LAG = 2
 TILE = 128
 F32, BF16 = jnp.float32, jnp.bfloat16
 
@@ -31,16 +32,15 @@
 
 def kernel(
     q_in, k_in, v_in, decay_in, gain_in, grad_in,
-    normed_out, gq_out, gk_out, gv_out,
+    normed, gq, gk, gv,
     q, k, v, decay, gain, grad,
-    normed, gq, gk, gv,
     cum, col, rise, fall, qdec, kdec, weights, probs, dscores,
     att, squares, crosses, datt, half, gk_part, gv_part,
     factor_send, factor_recv, row_factor,
     part_f, recv_f, rows_f, back_f, state_f,
     part_b, recv_b, rows_b, back_b, state_b,
     stats,
-    load_sem, store_sem,
+    load_sem,
     factor_ssem, factor_rsem, row_ssem, row_rsem,
     part_ssem, part_rsem, rows_ssem, rows_rsem, back_ssem, back_rsem,
     stat_ssem, stat_rsem,
@@ -120,7 +120,7 @@
             at = along_x(step)
             remote(target.at[at], target.at[at], ssem.at[at], rsem.at[at], at * Y + y, tp).wait_recv()
 
-    sent = []
+    first, second, third, fourth = [], [], [], []
 
     loads[0].wait()
     tokens = lax.broadcasted_iota(jnp.int32, (BLOCK, BLOCK), 0)
@@ -142,15 +142,15 @@
     for h in range(HEADS):
         lanes = slice(h * E, (h + 1) * E)
         kdec[:, lanes] = (k[:, lanes].astype(F32) * fall[h]).astype(BF16)
-        contrib = dot(kdec[:, lanes], v[:, lanes], TN)
-        part_f[2 * h] = contrib[:PART]
-        part_f[2 * h + 1] = contrib[PART:]
-
-    pl.semaphore_wait(barrier, Y + X + TP - 3)
-    sent += spread_y(lambda to: factor_send.at[to // 2], factor_recv, factor_ssem, factor_rsem)
-    sent += spread_y(lambda to: part_f.at[to], recv_f, part_ssem.at[0], part_rsem.at[0])
-    factor_recv[y] = factor_send[y // 2]
-    recv_f[y] = part_f[y]
+        part_f[h] = dot(kdec[:, lanes], v[:, lanes], TN).reshape(Y, PART, E)
+        if h == 0:
+            pl.semaphore_wait(barrier, Y + X + TP - 3)
+            first += spread_y(lambda to: factor_send, factor_recv, factor_ssem, factor_rsem)
+            factor_recv[y] = factor_send[...]
+        first += spread_y(
+            lambda to: part_f.at[h, to], recv_f.at[h], part_ssem.at[0, h], part_rsem.at[0, h]
+        )
+        recv_f[h, y] = part_f[h, y]
 
     loads[3].wait()
 
@@ -184,53 +184,61 @@
     for j in range(1, Y):
         product = product * factor_recv[j]
     row_factor[x] = product
-    sent += spread_x(row_factor.at[x], row_factor, row_ssem, row_rsem)
+    first += spread_x(row_factor.at[x], row_factor, row_ssem, row_rsem)
 
     def chain(order_y, order_x, before, recv, rows, back, state, n):
-        running = recv[order_y[0]]
-        back[order_y[0]] = jnp.zeros((PART, E), F32)
-        for j in order_y[1:]:
-            back[j] = running
-            running = factor_recv[j] * running + recv[j]
-        rows[x] = running
-        copies = spread_x(rows.at[x], rows, rows_ssem.at[n], rows_rsem.at[n])
-        if n == 0:
-            arrived_x(row_factor, row_rsem, row_ssem)
-        arrived_x(rows, rows_rsem.at[n], rows_ssem.at[n])
-        enter = jnp.zeros((PART, E), F32)
-        for i in order_x[:-1]:
-            enter = jnp.where(before(i), row_factor[i] * enter + rows[i], enter)
-        passed = enter
-        for j in order_y:
-            back[j] = back[j] + passed
-            passed = factor_recv[j] * passed
-        copies += spread_y(lambda to: back.at[to], state, back_ssem.at[n], back_rsem.at[n])
-        state[y] = back[y]
-        return copies
-
-    arrived_y(recv_f, part_rsem.at[0], part_ssem.at[0])
-    sent += chain(
+        to_rows, to_places = [], []
+        for turn in range(HEADS + LAG):
+            h = turn
+            if h < HEADS:
+                arrived_y(recv.at[h], part_rsem.at[n, h], part_ssem.at[n, h])
+                running = recv[h, order_y[0]]
+                back[h, order_y[0]] = jnp.zeros((PART, E), F32)
+                for j in order_y[1:]:
+                    back[h, j] = running
+                    running = factor_recv[j, h] * running + recv[h, j]
+                rows[h, x] = running
+                to_rows += spread_x(
+                    rows.at[h, x], rows.at[h], rows_ssem.at[n, h], rows_rsem.at[n, h]
+                )
+            if n == 0 and turn == LAG:
+                arrived_x(row_factor, row_rsem, row_ssem)
+            h = turn - LAG
+            if h >= 0:
+                arrived_x(rows.at[h], rows_rsem.at[n, h], rows_ssem.at[n, h])
+                enter = jnp.zeros((PART, E), F32)
+                for i in order_x[:-1]:
+                    enter = jnp.where(before(i), row_factor[i, h] * enter + rows[h, i], enter)
+                for j in order_y:
+                    back[h, j] = back[h, j] + enter
+                    enter = factor_recv[j, h] * enter
+                to_places += spread_y(
+                    lambda to: back.at[h, to], state.at[h], back_ssem.at[n, h], back_rsem.at[n, h]
+                )
+                state[h, y] = back[h, y]
+        return to_rows, to_places
+
+    to_rows, to_places = chain(
         list(range(Y)), list(range(X)), lambda i: i < x, recv_f, rows_f, back_f, state_f, 0
     )
+    first += to_rows
+    second += to_places
     loads[4].wait()
     loads[5].wait()
-    arrived_y(state_f, back_rsem.at[0], back_ssem.at[0])
-
-    def across(h, carry):
-        lanes = pl.ds(pl.multiple_of(h * E, E), E)
-        entering = state_f[pl.ds(2 * h, 2)].reshape(E, E).astype(BF16)
+    for copy in first:
+        copy.wait_send()
+
+    for h in range(HEADS):
+        lanes = slice(h * E, (h + 1) * E)
+        arrived_y(state_f.at[h], back_rsem.at[0, h], back_ssem.at[0, h])
+        entering = state_f[h].reshape(E, E).astype(BF16)
         half[h] = entering
         whole = att[:, lanes] + dot(qdec[:, lanes], entering, NN)
         att[:, lanes] = whole
         cotangent = gain[:, lanes] * grad[:, lanes].astype(F32)
-        first = h == 0
-        squares[...] = jnp.where(first, 0.0, squares[...]) + whole * whole
-        crosses[...] = jnp.where(first, 0.0, crosses[...]) + cotangent * whole
-        return carry
-
-    squares[...] = jnp.zeros((BLOCK, E), F32)
-    crosses[...] = jnp.zeros((BLOCK, E), F32)
-    lax.fori_loop(0, HEADS, across, 0)
+        square, cross = whole * whole, cotangent * whole
+        squares[...] = square if h == 0 else squares[...] + square
+        crosses[...] = cross if h == 0 else crosses[...] + cross
 
     own = jnp.concatenate(
         [
@@ -242,10 +250,10 @@
     stats[tp] = own
     for step in TP_STEPS:
         to = along_tp(step)
-        sent.append(
+        second.append(
             remote(stats.at[tp], stats.at[tp], stat_ssem.at[to], stat_rsem.at[tp], ctx, to)
         )
-        sent[-1].start()
+        second[-1].start()
     for step in TP_STEPS:
         at = along_tp(step)
         remote(stats.at[at], stats.at[at], stat_ssem.at[at], stat_rsem.at[at], ctx, at).wait_recv()
@@ -257,8 +265,8 @@
     squares[...] = columns(inverse_row)
     crosses[...] = columns(slope_row)
 
-    def cotangents(h, carry):
-        lanes = pl.ds(pl.multiple_of(h * E, E), E)
+    for h in range(HEADS):
+        lanes = slice(h * E, (h + 1) * E)
         inverse = squares[...]
         whole = att[:, lanes]
         scale = gain[:, lanes]
@@ -266,12 +274,11 @@
             inverse * (scale * grad[:, lanes].astype(F32)) - whole * crosses[...]
         ).astype(BF16)
         datt[:, lanes] = here
-        part_b[pl.ds(2 * h, 2)] = dot(qdec[:, lanes], here, TN).reshape(2, PART, E)
-        return carry
-
-    lax.fori_loop(0, HEADS, cotangents, 0)
-    sent += spread_y(lambda to: part_b.at[to], recv_b, part_ssem.at[1], part_rsem.at[1])
-    recv_b[y] = part_b[y]
+        part_b[h] = dot(qdec[:, lanes], here, TN).reshape(Y, PART, E)
+        third += spread_y(
+            lambda to: part_b.at[h, to], recv_b.at[h], part_ssem.at[1, h], part_rsem.at[1, h]
+        )
+        recv_b[h, y] = part_b[h, y]
 
     def backward(h, carry):
         lanes = pl.ds(pl.multiple_of(h * E, E), E)
@@ -293,36 +300,38 @@
         return carry
 
     lax.fori_loop(0, HEADS, backward, 0)
-    stores = [
-        pltpu.make_async_copy(src, dst, store_sem.at[n])
-        for n, (src, dst) in enumerate(
-            ((normed, normed_out), (gq, gq_out), (gk, gk_out), (gv, gv_out))
-        )
-    ]
-    stores[0].start()
-    stores[1].start()
-
-    arrived_y(recv_b, part_rsem.at[1], part_ssem.at[1])
-    sent += chain(
+    for copy in second:
+        copy.wait_send()
+
+    to_rows, to_places = chain(
         list(reversed(range(Y))), list(reversed(range(X))), lambda i: i > x,
         recv_b, rows_b, back_b, state_b, 1,
     )
-    arrived_y(state_b, back_rsem.at[1], back_ssem.at[1])
-
-    def finish(h, carry):
-        lanes = pl.ds(pl.multiple_of(h * E, E), E)
-        leaving = state_b[pl.ds(2 * h, 2)].reshape(E, E).astype(BF16)
+    third += to_rows
+    fourth += to_places
+    for copy in third:
+        copy.wait_send()
+    for h in range(HEADS):
+        lanes = slice(h * E, (h + 1) * E)
+        if h == HEADS - 1:
+            for copy in fourth:
+                copy.wait_send()
+        arrived_y(state_b.at[h], back_rsem.at[1, h], back_ssem.at[1, h])
+        leaving = state_b[h].reshape(E, E).astype(BF16)
         gk[:, lanes] = (
             gk_part[:, lanes] + fall[h] * dot(v[:, lanes], leaving, NT)
         ).astype(BF16)
         gv[:, lanes] = (gv_part[:, lanes] + dot(kdec[:, lanes], leaving, NN)).astype(BF16)
-        return carry
-
-    lax.fori_loop(0, HEADS, finish, 0)
-    stores[2].start()
-    stores[3].start()
-    for copy in sent:
-        copy.wait_send()
+
+
+def write(*refs):
+    sources, results, sem = refs[:4], refs[4:8], refs[8]
+    stores = [
+        pltpu.make_async_copy(src, dst, sem.at[n])
+        for n, (src, dst) in enumerate(zip(sources, results))
+    ]
+    for store in stores:
+        store.start()
     for store in stores:
         store.wait()
 
@@ -334,35 +343,48 @@
     head32 = pltpu.VMEM((HEADS, BLOCK, E), F32)
     one32 = pltpu.VMEM((BLOCK, E), F32)
     square = (HEADS, BLOCK, BLOCK)
-    parts = pltpu.VMEM((Y, PART, E), F32)
-    across = pltpu.VMEM((X, PART, E), F32)
+    parts = pltpu.VMEM((HEADS, Y, PART, E), F32)
+    across = pltpu.VMEM((HEADS, X, PART, E), F32)
     sem = pltpu.SemaphoreType.DMA
     chain = [parts, parts, across, parts, parts]
     anywhere = pl.BlockSpec(memory_space=pl.ANY)
-    return pl.pallas_call(
+    vmem = pl.BlockSpec(memory_space=pltpu.VMEM)
+    results = pl.pallas_call(
         kernel,
-        out_shape=(tile,) * 4,
+        out_shape=(pltpu.VMEM((BLOCK, HEADS * E), BF16),) * 4,
         in_specs=[anywhere] * 6,
-        out_specs=(anywhere,) * 4,
+        out_specs=(vmem,) * 4,
         scratch_shapes=[
             flat16, flat16, flat16,
             pltpu.VMEM((HEADS, BLOCK), F32), pltpu.VMEM((1, HEADS * E), F32), flat16,
-            flat16, flat16, flat16, flat16,
             pltpu.VMEM((HEADS, BLOCK), F32), head32, head32, head32, flat16, flat16,
             pltpu.VMEM(square, F32), pltpu.VMEM(square, BF16), pltpu.VMEM(square, BF16),
             flat32, one32, one32, flat16, pltpu.VMEM((HEADS, E, E), BF16), flat32, flat32,
-            pltpu.VMEM((HEADS, 1, TILE), F32), pltpu.VMEM((Y, 1, TILE), F32),
-            pltpu.VMEM((X, 1, TILE), F32),
+            pltpu.VMEM((HEADS, 1, TILE), F32), pltpu.VMEM((Y, HEADS, 1, TILE), F32),
+            pltpu.VMEM((X, HEADS, 1, TILE), F32),
             *chain, *chain,
             pltpu.VMEM((TP, 2, BLOCK), F32),
-            sem((6,)), sem((4,)),
+            sem((6,)),
             sem((Y,)), sem((Y,)), sem((X,)), sem((X,)),
-            sem((2, Y)), sem((2, Y)), sem((2, X)), sem((2, X)), sem((2, Y)), sem((2, Y)),
+            *[sem((2, HEADS, n)) for n in (Y, Y, X, X, Y, Y)],
             sem((TP,)), sem((TP,)),
         ],
-        compiler_params=pltpu.CompilerParams(collective_id=0, has_side_effects=True),
+        compiler_params=pltpu.CompilerParams(
+            collective_id=0,
+            has_side_effects=True,
+            vmem_limit_bytes=67043328 - 4 * BLOCK * HEADS * E * 2,
+        ),
         name="layer",
     )(queries, keys, values, log_decay, gain.reshape(1, -1), grad_out)
+    return pl.pallas_call(
+        write,
+        out_shape=(tile,) * 4,
+        in_specs=[vmem] * 4,
+        out_specs=(anywhere,) * 4,
+        scratch_shapes=[sem((4,))],
+        compiler_params=pltpu.CompilerParams(vmem_limit_bytes=16 * 2**20),
+        name="write",
+    )(*results)
 
 
 def solution(mesh):

time: 68.1 us -> 59 us (0.87)
  local copies, waits for them, and re-layouts: 5.18 us -> 0 us
  Pallas kernels: 62 us -> 57.8 us
    unnamed x10 -> x0, local copies, waits for them, and re-layouts: 5.18 us -> none
    pallas_call x1 -> x2, Pallas kernels: 62 us -> 57.8 us  [the longest x1 56.5 us: per_device(): pl.pallas_call(kernel, out_shape=(pltpu.VMEM((BLOCK, HEADS * E), BF16),)...]
where the time goes in v2:
time: 59 us; the launch traced here: 58.5 us
  Pallas kernels  57.8 us (98%)
  between operations  0.64 us (1%)
    pallas_call x1, Pallas kernels, per_device(): pl.pallas_call(kernel, out_shape=(pltpu.VMEM((BLOCK, HEADS * E), BF16),)...  56.5 us
    pallas_call x1, Pallas kernels, per_device(): pl.pallas_call(write, out_shape=(tile,) * 4, in_specs=[vmem] * 4, out_spe...  1.35 us

profile of v2, /device:TPU:1, one launch (start us, length us, event | category | flops | bytes accessed | tf_op | source)
XLA Modules:
  0.0 58.5 jit_solution(6588959473290560743)
XLA Ops:
  0.6 56.5 %layer.1 = (bf16[512,512]{1,0:T(8,128)(2,1)S(1)}, bf16[512,512]{1,0:T(8,128)(2,1)S(1)}, bf16[512,512]{1,0:T(8,128)(2,1)S(1)}, bf16[512,512]{1,0:T(8,128)(2,1)S(1)}) custom-call(bf16[512,512]{1,0:T(8,128)(2,1)} %q_in.1, bf16[512,512]{1,0:T(8,128)(2,1)} %k_in.1, bf16[512,512]{1,0:T(8,128)(2,1)} %v_in.1, f32[4,512]{1,0:T(4,128)} %decay_in.1, f32[1,512]{1,0:T(1,128)} %bitcast.1, ...), custom_call_target="tpu_custom_call" | custom-call | tf_op jit(solution)/shard_map/layer/pallas_call | solution.py:352
  57.1 1.3 %write.1 = (bf16[512,512]{1,0:T(8,128)(2,1)}, bf16[512,512]{1,0:T(8,128)(2,1)}, bf16[512,512]{1,0:T(8,128)(2,1)}, bf16[512,512]{1,0:T(8,128)(2,1)}) custom-call(bf16[512,512]{1,0:T(8,128)(2,1)S(1)} %get-tuple-element.8.refs_0_, bf16[512,512]{1,0:T(8,128)(2,1)S(1)} %get-tuple-element.9.refs_1_, bf16[512,512]{1,0:T(8,128)(2,1)S(1)} %get-tuple-element.10.refs_2_, ...), custom_call_target="tpu_custom_call" | custom-call | tf_op jit(solution)/shard_map/write/pallas_call | solution.py:379

commit v3 on v2

--- a/solution.py
+++ b/solution.py
@@ -10,10 +10,12 @@
 BLOCK = 512
 EPSILON = 1e-05
 
-X, Y, TP = 4, 8, 16
+X, Y, Z, TP = 4, 8, 8, 16
 HEADS = ATTENTION_HEADS // TP
 PART = E // Y
-LAG = 2
+GROUP = 2
+CHUNKS = HEADS // GROUP
+LAG = 1
 TILE = 128
 F32, BF16 = jnp.float32, jnp.bfloat16
 
@@ -39,14 +41,16 @@
     factor_send, factor_recv, row_factor,
     part_f, recv_f, rows_f, back_f, state_f,
     part_b, recv_b, rows_b, back_b, state_b,
-    stats,
+    pair, stats,
     load_sem,
     factor_ssem, factor_rsem, row_ssem, row_rsem,
     part_ssem, part_rsem, rows_ssem, rows_rsem, back_ssem, back_rsem,
-    stat_ssem, stat_rsem,
+    pair_sem, stat_ssem, stat_rsem,
 ):
     ctx, tp = lax.axis_index("ctx"), lax.axis_index("tp")
     x, y = ctx // Y, ctx % Y
+    z, core = tp // 2, tp % 2
+    other = z * 2 + 1 - core
 
     loads = [
         pltpu.make_async_copy(src, dst, load_sem.at[n])
@@ -63,12 +67,12 @@
     def along_x(step):
         return (x + step) % X
 
-    def along_tp(step):
-        return (tp + step) % TP
+    def along_z(step):
+        return (z + step) % Z
 
     Y_STEPS = (4, 3, 5, 2, 6, 1, 7)
     X_STEPS = (2, 1, 3)
-    TP_STEPS = (8, 9, 7, 10, 6, 11, 5, 12, 4, 13, 3, 14, 2, 15, 1)
+    Z_STEPS = (4, 3, 5, 2, 6, 1, 7)
 
     barrier = pltpu.get_barrier_semaphore()
     for step in Y_STEPS:
@@ -79,10 +83,11 @@
         pl.semaphore_signal(
             barrier, 1, device_id=(along_x(step) * Y + y, tp), device_id_type=pl.DeviceIdType.MESH
         )
-    for step in TP_STEPS:
+    for step in Z_STEPS:
         pl.semaphore_signal(
-            barrier, 1, device_id=(ctx, along_tp(step)), device_id_type=pl.DeviceIdType.MESH
-        )
+            barrier, 1, device_id=(ctx, along_z(step) * 2 + core), device_id_type=pl.DeviceIdType.MESH
+        )
+    pl.semaphore_signal(barrier, 1, device_id=(ctx, other), device_id_type=pl.DeviceIdType.MESH)
 
     def remote(src, dst, ssem, rsem, to_ctx, to_tp):
         return pltpu.make_async_remote_copy(
@@ -123,12 +128,18 @@
     first, second, third, fourth = [], [], [], []
 
     loads[0].wait()
-    tokens = lax.broadcasted_iota(jnp.int32, (BLOCK, BLOCK), 0)
-    until = lax.broadcasted_iota(jnp.int32, (BLOCK, BLOCK), 1)
+    tokens = lax.broadcasted_iota(jnp.int32, (TILE, TILE), 0)
+    until = lax.broadcasted_iota(jnp.int32, (TILE, TILE), 1)
     upper = jnp.where(tokens <= until, 1.0, 0.0).astype(F32)
-    cum[...] = lax.dot_general(
-        decay[...], upper, NN, precision=lax.Precision.HIGHEST, preferred_element_type=F32
-    )
+    before = jnp.zeros((HEADS, 1), F32)
+    for c in range(BLOCK // TILE):
+        place = slice(c * TILE, (c + 1) * TILE)
+        summed = before + lax.dot_general(
+            decay[:, place], upper, NN, precision=lax.Precision.HIGHEST,
+            preferred_element_type=F32,
+        )
+        cum[:, place] = summed
+        before = summed[:, TILE - 1 : TILE]
     for h in range(HEADS):
         row = cum[h : h + 1, :]
         total = row[:, BLOCK - 1 : BLOCK]
@@ -142,15 +153,17 @@
     for h in range(HEADS):
         lanes = slice(h * E, (h + 1) * E)
         kdec[:, lanes] = (k[:, lanes].astype(F32) * fall[h]).astype(BF16)
-        part_f[h] = dot(kdec[:, lanes], v[:, lanes], TN).reshape(Y, PART, E)
+        g, inner = h // GROUP, slice(h % GROUP * PART, (h % GROUP + 1) * PART)
+        part_f[g, :, inner] = dot(kdec[:, lanes], v[:, lanes], TN).reshape(Y, PART, E)
         if h == 0:
-            pl.semaphore_wait(barrier, Y + X + TP - 3)
+            pl.semaphore_wait(barrier, Y + X + Z - 2)
             first += spread_y(lambda to: factor_send, factor_recv, factor_ssem, factor_rsem)
             factor_recv[y] = factor_send[...]
-        first += spread_y(
-            lambda to: part_f.at[h, to], recv_f.at[h], part_ssem.at[0, h], part_rsem.at[0, h]
-        )
-        recv_f[h, y] = part_f[h, y]
+        if h % GROUP == GROUP - 1:
+            first += spread_y(
+                lambda to: part_f.at[g, to], recv_f.at[g], part_ssem.at[0, g], part_rsem.at[0, g]
+            )
+            recv_f[g, y] = part_f[g, y]
 
     loads[3].wait()
 
@@ -188,34 +201,41 @@
 
     def chain(order_y, order_x, before, recv, rows, back, state, n):
         to_rows, to_places = [], []
-        for turn in range(HEADS + LAG):
-            h = turn
-            if h < HEADS:
-                arrived_y(recv.at[h], part_rsem.at[n, h], part_ssem.at[n, h])
-                running = recv[h, order_y[0]]
-                back[h, order_y[0]] = jnp.zeros((PART, E), F32)
-                for j in order_y[1:]:
-                    back[h, j] = running
-                    running = factor_recv[j, h] * running + recv[h, j]
-                rows[h, x] = running
+        inners = [slice(i * PART, (i + 1) * PART) for i in range(GROUP)]
+        for turn in range(CHUNKS + LAG):
+            g = turn
+            if g < CHUNKS:
+                arrived_y(recv.at[g], part_rsem.at[n, g], part_ssem.at[n, g])
+                for i, inner in enumerate(inners):
+                    h = g * GROUP + i
+                    running = recv[g, order_y[0], inner]
+                    back[g, order_y[0], inner] = jnp.zeros((PART, E), F32)
+                    for j in order_y[1:]:
+                        back[g, j, inner] = running
+                        running = factor_recv[j, h] * running + recv[g, j, inner]
+                    rows[g, x, inner] = running
                 to_rows += spread_x(
-                    rows.at[h, x], rows.at[h], rows_ssem.at[n, h], rows_rsem.at[n, h]
+                    rows.at[g, x], rows.at[g], rows_ssem.at[n, g], rows_rsem.at[n, g]
                 )
             if n == 0 and turn == LAG:
                 arrived_x(row_factor, row_rsem, row_ssem)
-            h = turn - LAG
-            if h >= 0:
-                arrived_x(rows.at[h], rows_rsem.at[n, h], rows_ssem.at[n, h])
-                enter = jnp.zeros((PART, E), F32)
-                for i in order_x[:-1]:
-                    enter = jnp.where(before(i), row_factor[i, h] * enter + rows[h, i], enter)
-                for j in order_y:
-                    back[h, j] = back[h, j] + enter
-                    enter = factor_recv[j, h] * enter
+            g = turn - LAG
+            if g >= 0:
+                arrived_x(rows.at[g], rows_rsem.at[n, g], rows_ssem.at[n, g])
+                for i, inner in enumerate(inners):
+                    h = g * GROUP + i
+                    enter = jnp.zeros((PART, E), F32)
+                    for k in order_x[:-1]:
+                        enter = jnp.where(
+                            before(k), row_factor[k, h] * enter + rows[g, k, inner], enter
+                        )
+                    for j in order_y:
+                        back[g, j, inner] = back[g, j, inner] + enter
+                        enter = factor_recv[j, h] * enter
                 to_places += spread_y(
-                    lambda to: back.at[h, to], state.at[h], back_ssem.at[n, h], back_rsem.at[n, h]
+                    lambda to: back.at[g, to], state.at[g], back_ssem.at[n, g], back_rsem.at[n, g]
                 )
-                state[h, y] = back[h, y]
+                state[g, y] = back[g, y]
         return to_rows, to_places
 
     to_rows, to_places = chain(
@@ -230,8 +250,10 @@
 
     for h in range(HEADS):
         lanes = slice(h * E, (h + 1) * E)
-        arrived_y(state_f.at[h], back_rsem.at[0, h], back_ssem.at[0, h])
-        entering = state_f[h].reshape(E, E).astype(BF16)
+        g, inner = h // GROUP, slice(h % GROUP * PART, (h % GROUP + 1) * PART)
+        if h % GROUP == 0:
+            arrived_y(state_f.at[g], back_rsem.at[0, g], back_ssem.at[0, g])
+        entering = state_f[g, :, inner].reshape(E, E).astype(BF16)
         half[h] = entering
         whole = att[:, lanes] + dot(qdec[:, lanes], entering, NN)
         att[:, lanes] = whole
@@ -247,18 +269,26 @@
         ],
         axis=0,
     )
-    stats[tp] = own
-    for step in TP_STEPS:
-        to = along_tp(step)
+    pair[0] = own
+    second.append(remote(pair.at[0], pair.at[1], pair_sem.at[0], pair_sem.at[1], ctx, other))
+    second[-1].start()
+    second[-1].wait_recv()
+    stats[z] = own + pair[1]
+    for step in Z_STEPS:
+        to = along_z(step)
         second.append(
-            remote(stats.at[tp], stats.at[tp], stat_ssem.at[to], stat_rsem.at[tp], ctx, to)
+            remote(
+                stats.at[z], stats.at[z], stat_ssem.at[to], stat_rsem.at[z], ctx, to * 2 + core
+            )
         )
         second[-1].start()
-    for step in TP_STEPS:
-        at = along_tp(step)
-        remote(stats.at[at], stats.at[at], stat_ssem.at[at], stat_rsem.at[at], ctx, at).wait_recv()
+    for step in Z_STEPS:
+        at = along_z(step)
+        remote(
+            stats.at[at], stats.at[at], stat_ssem.at[at], stat_rsem.at[at], ctx, at * 2 + core
+        ).wait_recv()
     sums = stats[0]
-    for i in range(1, TP):
+    for i in range(1, Z):
         sums = sums + stats[i]
     inverse_row = lax.rsqrt(sums[0:1] / (ATTENTION_HEADS * E) + EPSILON)
     slope_row = inverse_row * inverse_row * inverse_row * sums[1:2] / (ATTENTION_HEADS * E)
@@ -274,11 +304,13 @@
             inverse * (scale * grad[:, lanes].astype(F32)) - whole * crosses[...]
         ).astype(BF16)
         datt[:, lanes] = here
-        part_b[h] = dot(qdec[:, lanes], here, TN).reshape(Y, PART, E)
-        third += spread_y(
-            lambda to: part_b.at[h, to], recv_b.at[h], part_ssem.at[1, h], part_rsem.at[1, h]
-        )
-        recv_b[h, y] = part_b[h, y]
+        g, inner = h // GROUP, slice(h % GROUP * PART, (h % GROUP + 1) * PART)
+        part_b[g, :, inner] = dot(qdec[:, lanes], here, TN).reshape(Y, PART, E)
+        if h % GROUP == GROUP - 1:
+            third += spread_y(
+                lambda to: part_b.at[g, to], recv_b.at[g], part_ssem.at[1, g], part_rsem.at[1, g]
+            )
+            recv_b[g, y] = part_b[g, y]
 
     def backward(h, carry):
         lanes = pl.ds(pl.multiple_of(h * E, E), E)
@@ -300,24 +332,23 @@
         return carry
 
     lax.fori_loop(0, HEADS, backward, 0)
-    for copy in second:
-        copy.wait_send()
-
     to_rows, to_places = chain(
         list(reversed(range(Y))), list(reversed(range(X))), lambda i: i > x,
         recv_b, rows_b, back_b, state_b, 1,
     )
     third += to_rows
     fourth += to_places
-    for copy in third:
+    for copy in second + third:
         copy.wait_send()
     for h in range(HEADS):
         lanes = slice(h * E, (h + 1) * E)
-        if h == HEADS - 1:
+        g, inner = h // GROUP, slice(h % GROUP * PART, (h % GROUP + 1) * PART)
+        if h == HEADS - GROUP:
             for copy in fourth:
                 copy.wait_send()
-        arrived_y(state_b.at[h], back_rsem.at[1, h], back_ssem.at[1, h])
-        leaving = state_b[h].reshape(E, E).astype(BF16)
+        if h % GROUP == 0:
+            arrived_y(state_b.at[g], back_rsem.at[1, g], back_ssem.at[1, g])
+        leaving = state_b[g, :, inner].reshape(E, E).astype(BF16)
         gk[:, lanes] = (
             gk_part[:, lanes] + fall[h] * dot(v[:, lanes], leaving, NT)
         ).astype(BF16)
@@ -343,8 +374,8 @@
     head32 = pltpu.VMEM((HEADS, BLOCK, E), F32)
     one32 = pltpu.VMEM((BLOCK, E), F32)
     square = (HEADS, BLOCK, BLOCK)
-    parts = pltpu.VMEM((HEADS, Y, PART, E), F32)
-    across = pltpu.VMEM((HEADS, X, PART, E), F32)
+    parts = pltpu.VMEM((CHUNKS, Y, GROUP * PART, E), F32)
+    across = pltpu.VMEM((CHUNKS, X, GROUP * PART, E), F32)
     sem = pltpu.SemaphoreType.DMA
     chain = [parts, parts, across, parts, parts]
     anywhere = pl.BlockSpec(memory_space=pl.ANY)
@@ -363,11 +394,11 @@
             pltpu.VMEM((HEADS, 1, TILE), F32), pltpu.VMEM((Y, HEADS, 1, TILE), F32),
             pltpu.VMEM((X, HEADS, 1, TILE), F32),
             *chain, *chain,
-            pltpu.VMEM((TP, 2, BLOCK), F32),
+            pltpu.VMEM((2, 2, BLOCK), F32), pltpu.VMEM((Z, 2, BLOCK), F32),
             sem((6,)),
             sem((Y,)), sem((Y,)), sem((X,)), sem((X,)),
-            *[sem((2, HEADS, n)) for n in (Y, Y, X, X, Y, Y)],
-            sem((TP,)), sem((TP,)),
+            *[sem((2, CHUNKS, n)) for n in (Y, Y, X, X, Y, Y)],
+            sem((2,)), sem((Z,)), sem((Z,)),
         ],
         compiler_params=pltpu.CompilerParams(
             collective_id=0,

time: 59 us -> 57.5 us (0.975)
  the two profiles are of different devices: /device:TPU:1 before, /device:TPU:2 now
where the time goes in v3:
time: 57.5 us; the launch traced here: 57.4 us
  Pallas kernels  56.7 us (99%)
  between operations  0.64 us (1%)
    pallas_call x1, Pallas kernels, per_device(): pl.pallas_call(kernel, out_shape=(pltpu.VMEM((BLOCK, HEADS * E), BF16),)...  55.4 us
    pallas_call x1, Pallas kernels, per_device(): pl.pallas_call(write, out_shape=(tile,) * 4, in_specs=[vmem] * 4, out_spe...  1.35 us

profile of v3, /device:TPU:2, one launch (start us, length us, event | category | flops | bytes accessed | tf_op | source)
XLA Modules:
  0.0 57.4 jit_solution(628028413745521310)
XLA Ops:
  0.6 55.4 %layer.1 = (bf16[512,512]{1,0:T(8,128)(2,1)S(1)}, bf16[512,512]{1,0:T(8,128)(2,1)S(1)}, bf16[512,512]{1,0:T(8,128)(2,1)S(1)}, bf16[512,512]{1,0:T(8,128)(2,1)S(1)}) custom-call(bf16[512,512]{1,0:T(8,128)(2,1)} %q_in.1, bf16[512,512]{1,0:T(8,128)(2,1)} %k_in.1, bf16[512,512]{1,0:T(8,128)(2,1)} %v_in.1, f32[4,512]{1,0:T(4,128)} %decay_in.1, f32[1,512]{1,0:T(1,128)} %bitcast.1, ...), custom_call_target="tpu_custom_call" | custom-call | tf_op jit(solution)/shard_map/layer/pallas_call | solution.py:383
  56.0 1.3 %write.1 = (bf16[512,512]{1,0:T(8,128)(2,1)}, bf16[512,512]{1,0:T(8,128)(2,1)}, bf16[512,512]{1,0:T(8,128)(2,1)}, bf16[512,512]{1,0:T(8,128)(2,1)}) custom-call(bf16[512,512]{1,0:T(8,128)(2,1)S(1)} %get-tuple-element.8.refs_0_, bf16[512,512]{1,0:T(8,128)(2,1)S(1)} %get-tuple-element.9.refs_1_, bf16[512,512]{1,0:T(8,128)(2,1)S(1)} %get-tuple-element.10.refs_2_, ...), custom_call_target="tpu_custom_call" | custom-call | tf_op jit(solution)/shard_map/write/pallas_call | solution.py:410

commit v4 on v3

--- a/solution.py
+++ b/solution.py
@@ -36,7 +36,7 @@
     q_in, k_in, v_in, decay_in, gain_in, grad_in,
     normed, gq, gk, gv,
     q, k, v, decay, gain, grad,
-    cum, col, rise, fall, qdec, kdec, weights, probs, dscores,
+    cum, rise, fall, qdec, kdec, weights, probs, dscores,
     att, squares, crosses, datt, half, gk_part, gv_part,
     factor_send, factor_recv, row_factor,
     part_f, recv_f, rows_f, back_f, state_f,
@@ -141,18 +141,16 @@
         cum[:, place] = summed
         before = summed[:, TILE - 1 : TILE]
     for h in range(HEADS):
-        row = cum[h : h + 1, :]
-        total = row[:, BLOCK - 1 : BLOCK]
+        total = cum[h : h + 1, BLOCK - 1 : BLOCK]
         factor_send[h] = jnp.exp(jnp.broadcast_to(total, (1, TILE)))
-        wide = columns(row)
-        col[h] = wide
-        rise[h] = jnp.exp(wide)
-        fall[h] = jnp.exp(total - wide)
     loads[1].wait()
     loads[2].wait()
     for h in range(HEADS):
         lanes = slice(h * E, (h + 1) * E)
-        kdec[:, lanes] = (k[:, lanes].astype(F32) * fall[h]).astype(BF16)
+        row = cum[h : h + 1, :]
+        drop = columns(jnp.exp(row[:, BLOCK - 1 : BLOCK] - row))
+        fall[h] = drop
+        kdec[:, lanes] = (k[:, lanes].astype(F32) * drop).astype(BF16)
         g, inner = h // GROUP, slice(h % GROUP * PART, (h % GROUP + 1) * PART)
         part_f[g, :, inner] = dot(kdec[:, lanes], v[:, lanes], TN).reshape(Y, PART, E)
         if h == 0:
@@ -169,12 +167,15 @@
 
     def inside(h, carry):
         lanes = pl.ds(pl.multiple_of(h * E, E), E)
-        qdec[:, lanes] = (q[:, lanes].astype(F32) * rise[h]).astype(BF16)
         row = cum[pl.ds(h, 1), :]
+        wide = columns(row)
+        grow = jnp.exp(wide)
+        rise[h] = grow
+        qdec[:, lanes] = (q[:, lanes].astype(F32) * grow).astype(BF16)
         for r in range(BLOCK // TILE):
             rows, width = slice(r * TILE, (r + 1) * TILE), (r + 1) * TILE
             scores = dot(q[rows, lanes], k[:width, lanes], NT)
-            mine = col[h, rows, :]
+            mine = wide[rows]
             pieces = []
             for c in range(r + 1):
                 spread = mine - row[:, c * TILE : (c + 1) * TILE]
@@ -388,7 +389,7 @@
         scratch_shapes=[
             flat16, flat16, flat16,
             pltpu.VMEM((HEADS, BLOCK), F32), pltpu.VMEM((1, HEADS * E), F32), flat16,
-            pltpu.VMEM((HEADS, BLOCK), F32), head32, head32, head32, flat16, flat16,
+            pltpu.VMEM((HEADS, BLOCK), F32), head32, head32, flat16, flat16,
             pltpu.VMEM(square, F32), pltpu.VMEM(square, BF16), pltpu.VMEM(square, BF16),
             flat32, one32, one32, flat16, pltpu.VMEM((HEADS, E, E), BF16), flat32, flat32,
             pltpu.VMEM((HEADS, 1, TILE), F32), pltpu.VMEM((Y, HEADS, 1, TILE), F32),

time: 57.5 us -> 58.1 us (1.010)
  the two profiles are of different devices: /device:TPU:2 before, /device:TPU:1 now
where the time goes in v4:
time: 58.1 us; the launch traced here: 57.6 us
  Pallas kernels  56.9 us (98%)
  between operations  0.64 us (1%)
    pallas_call x1, Pallas kernels, per_device(): pl.pallas_call(kernel, out_shape=(pltpu.VMEM((BLOCK, HEADS * E), BF16),)...  55.6 us
    pallas_call x1, Pallas kernels, per_device(): pl.pallas_call(write, out_shape=(tile,) * 4, in_specs=[vmem] * 4, out_spe...  1.35 us

profile of v4, /device:TPU:1, one launch (start us, length us, event | category | flops | bytes accessed | tf_op | source)
XLA Modules:
  0.0 57.6 jit_solution(2797088000349404897)
XLA Ops:
  0.6 55.6 %layer.1 = (bf16[512,512]{1,0:T(8,128)(2,1)S(1)}, bf16[512,512]{1,0:T(8,128)(2,1)S(1)}, bf16[512,512]{1,0:T(8,128)(2,1)S(1)}, bf16[512,512]{1,0:T(8,128)(2,1)S(1)}) custom-call(bf16[512,512]{1,0:T(8,128)(2,1)} %q_in.1, bf16[512,512]{1,0:T(8,128)(2,1)} %k_in.1, bf16[512,512]{1,0:T(8,128)(2,1)} %v_in.1, f32[4,512]{1,0:T(4,128)} %decay_in.1, f32[1,512]{1,0:T(1,128)} %bitcast.1, ...), custom_call_target="tpu_custom_call" | custom-call | tf_op jit(solution)/shard_map/layer/pallas_call | solution.py:384
  56.2 1.3 %write.1 = (bf16[512,512]{1,0:T(8,128)(2,1)}, bf16[512,512]{1,0:T(8,128)(2,1)}, bf16[512,512]{1,0:T(8,128)(2,1)}, bf16[512,512]{1,0:T(8,128)(2,1)}) custom-call(bf16[512,512]{1,0:T(8,128)(2,1)S(1)} %get-tuple-element.8.refs_0_, bf16[512,512]{1,0:T(8,128)(2,1)S(1)} %get-tuple-element.9.refs_1_, bf16[512,512]{1,0:T(8,128)(2,1)S(1)} %get-tuple-element.10.refs_2_, ...), custom_call_target="tpu_custom_call" | custom-call | tf_op jit(solution)/shard_map/write/pallas_call | solution.py:411
